TPU v7x, 32 devices: a whole 2x2x4 slice. The times are simulated.
32 devices in a mesh: grid: 8 (over y, x, core), sub: 4 (over z).
Axes of the slice: x: 2, y: 2, z: 4, core: 2. Of those that a mesh axis runs over, the one named last changes fastest.
Arguments:
- grid_x: bfloat16 [65536, 512], P(('grid', 'sub')), may hold values from -6 to 6
- mesh_h: bfloat16 [2048, 512], P(('grid', 'sub')), may hold values from -6 to 6
- gain_grid: float32 [512], replicated, may hold values from 0.1 to 1.9
- gain_mesh: float32 [512], replicated, may hold values from 0.1 to 1.9
- w_query: bfloat16 [512, 512], replicated, may hold values from -0.25 to 0.25
- w_key: bfloat16 [512, 512], replicated, may hold values from -0.25 to 0.25
- w_value: bfloat16 [512, 512], replicated, may hold values from -0.25 to 0.25
- w_out: bfloat16 [512, 512], replicated, may hold values from -0.25 to 0.25
- edge_bias: float32 [2048, 384], P(('grid', 'sub')), may hold values from -9 to 300
- neighbours: int32 [2048, 96], P(('grid', 'sub')), may hold values from 0 to 767, as said below
- valid: int32 [2048, 96], P(('grid', 'sub')), may hold values from 0 to 1, as said below
- send_rows: int32 [32, 3, 4, 64], P(('grid', 'sub')), may hold values from 0 to 2047, as said below
- out_grad: bfloat16 [2048, 512], P(('grid', 'sub')), may hold values from -24 to 24
Outputs:
- mesh_out: bfloat16 [2048, 512], P(('grid', 'sub'))
- mesh_grad: bfloat16 [2048, 512], P(('grid', 'sub'))
- grid_grad: bfloat16 [65536, 512], P(('grid', 'sub'))
- weight_grads: float32 [4, 512, 512], replicated
Inputs may be any that keep to these rules, and one draw needn't show every extreme that they name: `send_rows`: for each source device, slab offset and destination sub index the 64 local rows are distinct; rows sent to the slab below (o = 0) lie in the lower half of the device's 2048 rows, rows sent to the slab above (o = 2) in the upper half. `neighbours`: a slot (o * 4 + s) * 64 + t names row t of what device s of slab g - o + 1 sends to the node's device; slots of slabs outside the grid are never named; the 96 entries of a node are distinct; some slots are named by no node. The first two edges of every node are valid.
All inputs are finite; a program needn't handle non-finite values.
Results may differ from a plain program's by a relative error of at most 0.009.
Values may be sent and summed in bfloat16 or wider, within the bound.
A program may use at most 128 MiB of HBM per device.

v0:
```python
import jax
import jax.numpy as jnp
from jax import lax
from jax.sharding import PartitionSpec as P

EPSILON = 1e-06
NEG_FILL = -1e30


def from_behind(block, axis, distance):
    devices = range(lax.axis_size(axis))
    route = [(i - distance, i) for i in devices if i - distance in devices]
    return lax.ppermute(block, axis, route)


def normalize(values_in, gain_row):
    widened = values_in.astype(jnp.float32)
    factor = lax.rsqrt(jnp.mean(widened * widened, axis=-1, keepdims=True) + EPSILON)
    return (widened, factor, (widened * factor * gain_row).astype(jnp.bfloat16))


def normalize_back(widened, factor, gain_row, upstream):
    scaled = gain_row * upstream
    inner_mean = jnp.mean(widened * scaled, axis=-1, keepdims=True)
    return factor * scaled - widened * factor**3 * inner_mean


def shards(
    grid_x,
    mesh_h,
    gain_grid,
    gain_mesh,
    w_query,
    w_key,
    w_value,
    w_out,
    edge_bias,
    neighbours,
    valid,
    send_rows,
    out_grad,
):
    point_count, model_width = grid_x.shape
    node_count = mesh_h.shape[0]
    sub_count = send_rows.shape[2]
    slots_per = send_rows.shape[3]
    block = sub_count * slots_per
    slot_count = 3 * block
    fanout = neighbours.shape[1]
    head_count = edge_bias.shape[1] // fanout
    head_width = model_width // head_count
    logit_scale = head_width ** (-0.5)
    w_pair = jnp.concatenate([w_key, w_value], axis=1)
    grid_wide, grid_factor, grid_normed = normalize(grid_x, gain_grid)
    flat_rows = send_rows[0].reshape(slot_count)
    send_match = flat_rows[:, None] == jnp.arange(point_count, dtype=jnp.int32)[None, :]
    send_onehot = send_match.astype(jnp.bfloat16)
    sent_normed = jnp.dot(send_onehot, grid_normed, preferred_element_type=jnp.float32).astype(
        jnp.bfloat16
    )
    packet = sent_normed.reshape(3, sub_count, slots_per, model_width)
    packet_width = packet.shape[3]
    mixed = lax.all_to_all(packet, "sub", split_axis=1, concat_axis=1, tiled=True).reshape(
        3, block, packet_width
    )
    pieces = []
    for offset in (0, 1, 2):
        piece = mixed[offset]
        if offset != 1:
            piece = from_behind(piece, "grid", offset - 1)
        pieces.append(piece)
    arrived = jnp.concatenate(pieces, axis=0)
    recv_pair = jnp.dot(arrived, w_pair, preferred_element_type=jnp.float32).astype(jnp.bfloat16)
    slot_onehot = (
        neighbours[:, :, None] == jnp.arange(slot_count, dtype=jnp.int32)[None, None, :]
    ).astype(jnp.bfloat16)
    edge_pair = jnp.einsum(
        "gjc,ce->gje", slot_onehot, recv_pair, preferred_element_type=jnp.float32
    ).astype(jnp.bfloat16)
    edge_keys = edge_pair[:, :, :model_width].reshape(node_count, fanout, head_count, head_width)
    edge_values = edge_pair[:, :, model_width:].reshape(node_count, fanout, head_count, head_width)
    mesh_wide, mesh_factor, mesh_normed = normalize(mesh_h, gain_mesh)
    queries = (
        jnp.dot(mesh_normed, w_query, preferred_element_type=jnp.float32) * logit_scale
    ).astype(jnp.bfloat16)
    query_head_rows = queries.reshape(node_count, head_count, head_width)
    score_matrix = jnp.einsum(
        "gip,gjip->gij", query_head_rows, edge_keys, preferred_element_type=jnp.float32
    ) + edge_bias.reshape(node_count, head_count, fanout)
    live_mask = (valid == 1)[:, None, :]
    row_peak = jnp.max(jnp.where(live_mask, score_matrix, NEG_FILL), axis=2, keepdims=True)
    exp_terms = jnp.exp(jnp.where(live_mask, score_matrix - row_peak, NEG_FILL))
    attn_probs = exp_terms / jnp.sum(exp_terms, axis=2, keepdims=True)
    probabilities_batch = attn_probs.astype(jnp.bfloat16)
    attended_rows = (
        jnp.einsum(
            "gij,gjik->gik", probabilities_batch, edge_values, preferred_element_type=jnp.float32
        )
        .reshape(node_count, model_width)
        .astype(jnp.bfloat16)
    )
    mesh_out = (
        mesh_wide + jnp.dot(attended_rows, w_out, preferred_element_type=jnp.float32)
    ).astype(jnp.bfloat16)
    grad_wo = jnp.einsum("md,me->de", attended_rows, out_grad, preferred_element_type=jnp.float32)
    att_grad = jnp.einsum("me,de->md", out_grad, w_out, preferred_element_type=jnp.float32).astype(
        jnp.bfloat16
    )
    head_gradient = att_grad.reshape(node_count, head_count, head_width)
    probability_gradient = jnp.einsum(
        "gip,gjip->gij", head_gradient, edge_values, preferred_element_type=jnp.float32
    )
    score_gradient = (
        attn_probs
        * (probability_gradient - jnp.sum(attn_probs * probability_gradient, axis=2, keepdims=True))
    ).astype(jnp.bfloat16)
    query_gradient = (
        (
            jnp.einsum(
                "gij,gjik->gik", score_gradient, edge_keys, preferred_element_type=jnp.float32
            )
            * logit_scale
        )
        .reshape(node_count, model_width)
        .astype(jnp.bfloat16)
    )
    dense_score_gradient = jnp.einsum(
        "gij,gjc->gic", score_gradient, slot_onehot, preferred_element_type=jnp.float32
    ).astype(jnp.bfloat16)
    dense_probabilities = jnp.einsum(
        "gij,gjc->gic", probabilities_batch, slot_onehot, preferred_element_type=jnp.float32
    ).astype(jnp.bfloat16)
    key_part = jnp.einsum(
        "uza,uzt->azt", dense_score_gradient, query_head_rows, preferred_element_type=jnp.float32
    ).reshape(slot_count, model_width)
    value_part = jnp.einsum(
        "uza,uzt->azt", dense_probabilities, head_gradient, preferred_element_type=jnp.float32
    ).reshape(slot_count, model_width)
    back_packet = (
        jnp.concatenate([key_part, value_part], axis=1)
        .astype(jnp.bfloat16)
        .reshape(3, block, 2 * model_width)
    )
    home_pieces = []
    for offset in (0, 1, 2):
        piece = back_packet[offset]
        if offset != 1:
            piece = from_behind(piece, "grid", 1 - offset)
        home_pieces.append(piece)
    home = jnp.stack(home_pieces)
    home = home.reshape(3, sub_count, slots_per, 2 * model_width)
    returned = lax.all_to_all(home, "sub", split_axis=1, concat_axis=1, tiled=True).reshape(
        slot_count, 2 * model_width
    )
    pair_grads = jnp.einsum("sd,se->de", sent_normed, returned, preferred_element_type=jnp.float32)
    slot_back = jnp.einsum("se,de->sd", returned, w_pair, preferred_element_type=jnp.float32)
    normed_grad = jnp.einsum(
        "sp,sd->pd",
        send_match.astype(jnp.float32),
        slot_back,
        precision=lax.Precision.HIGHEST,
        preferred_element_type=jnp.float32,
    )
    grid_grad = normalize_back(grid_wide, grid_factor, gain_grid, normed_grad).astype(jnp.bfloat16)
    grad_wq = jnp.einsum(
        "md,me->de", mesh_normed, query_gradient, preferred_element_type=jnp.float32
    )
    mesh_normed_grad = jnp.einsum(
        "me,de->md", query_gradient, w_query, preferred_element_type=jnp.float32
    )
    mesh_grad = (
        out_grad.astype(jnp.float32)
        + normalize_back(mesh_wide, mesh_factor, gain_mesh, mesh_normed_grad)
    ).astype(jnp.bfloat16)
    local_grads = jnp.stack(
        [grad_wq, pair_grads[:, :model_width], pair_grads[:, model_width:], grad_wo]
    )
    weight_grads = lax.psum(local_grads, ("grid", "sub"))
    return (mesh_out, mesh_grad, grid_grad, weight_grads)


def solution(mesh):
    in_specs = (
        P(("grid", "sub"), None),
        P(("grid", "sub"), None),
        P(),
        P(),
        P(),
        P(),
        P(),
        P(),
        P(("grid", "sub"), None),
        P(("grid", "sub"), None),
        P(("grid", "sub"), None),
        P(("grid", "sub"), None, None, None),
        P(("grid", "sub"), None),
    )
    out_specs = (P(("grid", "sub"), None), P(("grid", "sub"), None), P(("grid", "sub"), None), P())
    return jax.shard_map(shards, mesh=mesh, in_specs=in_specs, out_specs=out_specs, check_vma=False)
```

profile of v0, /device:TPU:0, one launch (start us, length us, event | category | flops | bytes accessed | tf_op | source)
XLA Modules:
  0.0 303.4 jit_solution(8482572767754308976)
XLA Ops:
  7.2 3.0 copy.27
  10.8 2.0 fusion.35
  14.6 6.3 %all-to-all-start = ((bf16[3,4,64,512]{3,2,0,1:T(8,128)(2,1)}), bf16[3,4,64,512]{3,2,0,1:T(8,128)(2,1)S(1)}, u32[]{:S(2)}, u32[]{:S(2)}) async-start(bf16[3,4,64,512]{3,2,0,1:T(8,128)(2,1)} %copy.28), calls=%async_computation | async-start | bytes 1572864 | tf_op jit(solution)/shard_map/all_to_all | solution.py:63
  24.1 17.0 %all-to-all-done = bf16[3,4,64,512]{3,2,0,1:T(8,128)(2,1)S(1)} async-done(((bf16[3,4,64,512]{3,2,0,1:T(8,128)(2,1)}), bf16[3,4,64,512]{3,2,0,1:T(8,128)(2,1)S(1)}, u32[]{:S(2)}, u32[]{:S(2)}) %all-to-all-start) | async-done | bytes 786464 | tf_op jit(solution)/shard_map/all_to_all | solution.py:63
  42.4 3.2 %collective-permute-start.1 = (bf16[256,512]{1,0:T(8,128)(2,1)S(1)}, bf16[256,512]{1,0:T(8,128)(2,1)S(1)}, u32[]{:S(2)}, u32[]{:S(2)}) collective-permute-start(bf16[256,512]{1,0:T(8,128)(2,1)S(1)} %bitcast.119), channel_id=1, source_target_pairs={{0,4},{4,8},{8,12},{12,16},{16,20},{20,24},{24,28},{1,5},{5,9},{9,... | collective-permute-start | bytes 786440 | tf_op jit(solution)/shard_map/ppermute | solution.py:13
  46.8 2.2 fusion.123
  49.0 11.4 %fusion.7 = bf16[64,96,1024]{2,1,0:T(8,128)(2,1)S(1)} fusion(s32[64,96]{1,0:T(8,128)} %param.22, bf16[768,1024,1]{1,0,2:T(8,128)(2,1)S(1)} %fusion.123), kind=kOutput, calls=%fused_computation.12 | convolution fusion | flops 9674686464 | bytes 14180352 | tf_op jit(solution)/shard_map/gjc,ce->gje/dot_general | solution.py:77
  60.5 3.7 %slice_bitcast_fusion.1 = (bf16[64,12,4,8,128]{4,3,2,1,0:T(8,128)(2,1)S(1)}, bf16[64,12,4,8,128]{4,3,2,1,0:T(8,128)(2,1)S(1)}) fusion(bf16[64,96,1024]{2,1,0:T(8,128)(2,1)S(1)} %fusion.7), kind=kLoop, calls=%fused_computation.22 | loop fusion | bytes 25165824
  64.2 3.3 %fusion.14 = f32[64,4,1,96]{3,2,1,0:T(1,128)S(1)} fusion(bf16[64,4,128,1]{2,3,1,0:T(2,128)(2,1)S(1)} %reshape.124, bf16[64,12,4,8,128]{4,3,2,1,0:T(8,128)(2,1)S(1)} %get-tuple-element.16), kind=kOutput, calls=%fused_computation.19 | convolution fusion | flops 6291456 | bytes 6455296 | tf_op jit(solution)/shard_map/gip,gjip->gij/dot_general | solution.py:87
  67.6 3.3 %fusion.8 = f32[64,4,1,96]{3,2,1,0:T(1,128)S(1)} fusion(bf16[64,4,128,1]{2,3,1,0:T(2,128)(2,1)S(1)} %reshape.126, bf16[64,12,4,8,128]{4,3,2,1,0:T(8,128)(2,1)S(1)} %get-tuple-element.17), kind=kOutput, calls=%fused_computation.13 | convolution fusion | flops 6291456 | bytes 6455296 | tf_op jit(solution)/shard_map/gip,gjip->gij/dot_general | solution.py:110
  71.2 3.6 %fusion.39 = bf16[64,4,768]{2,1,0:T(4,128)(2,1)S(1)} fusion(s32[64,96]{1,0:T(8,128)S(1)} %copy-done.29, f32[64,4,96]{2,1,0:T(4,128)S(1)} %get-tuple-element.33, f32[64,4]{1,0:T(8,128)S(1)} %get-tuple-element.32), kind=kOutput, calls=%fused_computation.55 | convolution fusion | flops 42713088 | bytes 517120 | tf_op jit(solution)/shard_map/gij,gjc->gic/dot_general | solution.py:130
  75.8 3.5 %fusion.38 = bf16[64,4,768]{2,1,0:T(4,128)(2,1)S(1)} fusion(bf16[64,4,96]{2,1,0:T(4,128)(2,1)S(1)} %get-tuple-element.26, s32[64,96]{1,0:T(8,128)S(1)} %copy-done.29), kind=kOutput, calls=%fused_computation.54 | convolution fusion | flops 42663936 | bytes 466944 | tf_op jit(solution)/shard_map/gij,gjc->gic/dot_general | solution.py:127
  81.0 5.0 %collective-permute-start.2 = (bf16[256,1024]{1,0:T(8,128)(2,1)S(1)}, bf16[256,1024]{1,0:T(8,128)(2,1)S(1)}, u32[]{:S(2)}, u32[]{:S(2)}) collective-permute-start(bf16[256,1024]{1,0:T(8,128)(2,1)S(1)} %get-tuple-element.20), channel_id=1, source_target_pairs={{0,4},{4,8},{8,12},{12,16},{16,20},{20,24},{24,28},{1,5},{5,9},{9,... | collective-permute-start | bytes 1572872 | tf_op jit(solution)/shard_map/ppermute | solution.py:13
  87.5 4.3 %collective-permute-done.3 = bf16[256,1024]{1,0:T(8,128)(2,1)S(1)} collective-permute-done((bf16[256,1024]{1,0:T(8,128)(2,1)S(1)}, bf16[256,1024]{1,0:T(8,128)(2,1)S(1)}, u32[]{:S(2)}, u32[]{:S(2)}) %collective-permute-start.3) | collective-permute-done | bytes 524320 | tf_op jit(solution)/shard_map/ppermute | solution.py:13
  93.2 4.4 %all-to-all-start.1 = ((bf16[3,4,64,1024]{3,2,0,1:T(8,128)(2,1)}), bf16[3,4,64,1024]{3,2,0,1:T(8,128)(2,1)}, u32[]{:S(2)}, u32[]{:S(2)}) async-start(bf16[3,4,64,1024]{3,2,0,1:T(8,128)(2,1)} %copy.35), calls=%async_computation.1 | async-start | bytes 3145728 | tf_op jit(solution)/shard_map/all_to_all | solution.py:152
  97.9 4.7 %fusion.10 = f32[64,4,1,128]{3,2,1,0:T(1,128)S(1)} fusion(bf16[64,12,4,8,128]{4,3,2,1,0:T(8,128)(2,1)} %copy-done.2, bf16[64,4,96,1]{2,1,0,3:T(4,128)(2,1)S(1)} %copy-done.16), kind=kOutput, calls=%fused_computation.15 | convolution fusion | flops 6291456 | bytes 6471680 | tf_op jit(solution)/shard_map/gij,gjik->gik/dot_general | solution.py:96
  106.5 24.3 %all-to-all-done.1 = bf16[3,4,64,1024]{3,2,0,1:T(8,128)(2,1)} async-done(((bf16[3,4,64,1024]{3,2,0,1:T(8,128)(2,1)}), bf16[3,4,64,1024]{3,2,0,1:T(8,128)(2,1)}, u32[]{:S(2)}, u32[]{:S(2)}) %all-to-all-start.1) | async-done | bytes 1572896 | tf_op jit(solution)/shard_map/all_to_all | solution.py:152
  134.2 2.5 pad_maximum_fusion
  138.8 2.7 fusion.93
  141.6 6.1 %fusion.28 = (f32[2048]{0:T(1024)S(1)}, f32[2048,512]{0,1:T(8,128)S(1)}) fusion(bf16[2048,512]{0,1:T(8,128)(2,1)S(1)} %copy-done.4, f32[512]{0:T(512)S(1)} %copy-done.27, f32[768,512]{1,0:T(8,128)S(1)} %fusion.93, s32[768]{0:T(1024)S(1)} %copy-done.25), kind=kOutput, calls=%fused_computation.36 | convolution fusion | flops 9669441536 | bytes 7877632 | tf_op jit(solution)/shard_map/sp,sd->pd/dot_general | solution.py:157
  147.7 2.6 fusion.27
  150.3 3.9 %copy.37 = bf16[2048,512]{1,0:T(8,128)(2,1)} copy(bf16[2048,512]{0,1:T(8,128)(2,1)} %fusion.27) | data formatting | bytes 4194304
  154.2 137.7 %all-reduce.2.cloned.1.call-done = f32[4,512,512]{2,1,0:T(8,128)} async-done(((f32[4,512,512]{2,1,0:T(8,128)}), f32[4,512,512]{2,1,0:T(8,128)}) %all-reduce.2.cloned.1.call-update) | async-done | bytes 4194320 | tf_op jit(solution)/shard_map/psum | solution.py:178
  291.9 4.6 %copy.106 = f32[4,512,512]{2,1,0:T(8,128)} copy(f32[4,512,512]{2,1,0:T(8,128)} %all-reduce.2.cloned.1.call-done) | data formatting | bytes 8388608
  (110 shorter events, 23.4 us)
Async XLA Ops:
  7.2 16.6 %copy-start = (bf16[512,512]{1,0:T(8,128)(2,1)S(1)}, bf16[512,512]{1,0:T(8,128)(2,1)}, u32[]{:S(2)}) copy-start(bf16[512,512]{1,0:T(8,128)(2,1)} %param.17) | copy-start | bytes 1572868
  10.8 10.2 %copy-start.6 = (bf16[64,512]{1,0:T(8,128)(2,1)S(1)}, bf16[64,512]{1,0:T(8,128)(2,1)}, u32[]{:S(2)}) copy-start(bf16[64,512]{1,0:T(8,128)(2,1)} %param.14) | copy-start | bytes 196612
  12.8 10.7 %copy-start.7 = (bf16[512,512]{1,0:T(8,128)(2,1)S(1)}, bf16[512,512]{1,0:T(8,128)(2,1)}, u32[]{:S(2)}) copy-start(bf16[512,512]{1,0:T(8,128)(2,1)} %param.20) | copy-start | bytes 1572868
  12.8 10.7 %copy-start.11 = (bf16[64,512]{1,0:T(8,128)(2,1)S(1)}, bf16[64,512]{1,0:T(8,128)(2,1)}, u32[]{:S(2)}) copy-start(bf16[64,512]{1,0:T(8,128)(2,1)} %param.25) | copy-start | bytes 196612
  13.7 10.1 %copy-start.18 = (f32[512]{0:T(512)S(1)}, f32[512]{0:T(512)}, u32[]{:S(2)}) copy-start(f32[512]{0:T(512)} %param.16) | copy-start | bytes 6148
  13.7 32.0 %copy-start.12 = (bf16[512,512]{1,0:T(8,128)(2,1)S(1)}, bf16[512,512]{1,0:T(8,128)(2,1)}, u32[]{:S(2)}) copy-start(bf16[512,512]{1,0:T(8,128)(2,1)} %param.19) | copy-start | bytes 1572868
  13.7 32.9 %copy-start.13 = (f32[64,384]{1,0:T(8,128)S(1)}, f32[64,384]{1,0:T(8,128)}, u32[]{:S(2)}) copy-start(f32[64,384]{1,0:T(8,128)} %param.21) | copy-start | bytes 294916
  13.7 33.1 %copy-start.17 = (s32[64,96]{1,0:T(8,128)S(1)}, s32[64,96]{1,0:T(8,128)}, u32[]{:S(2)}) copy-start(s32[64,96]{1,0:T(8,128)} %param.23) | copy-start | bytes 73732
  14.6 26.5 %all-to-all-start = ((bf16[3,4,64,512]{3,2,0,1:T(8,128)(2,1)}), bf16[3,4,64,512]{3,2,0,1:T(8,128)(2,1)S(1)}, u32[]{:S(2)}, u32[]{:S(2)}) async-start(bf16[3,4,64,512]{3,2,0,1:T(8,128)(2,1)} %copy.28), calls=%async_computation | async-start | bytes 1572864 | tf_op jit(solution)/shard_map/all_to_all | solution.py:63
  41.1 5.7 %collective-permute-start = (bf16[256,512]{1,0:T(8,128)(2,1)S(1)}, bf16[256,512]{1,0:T(8,128)(2,1)S(1)}, u32[]{:S(2)}, u32[]{:S(2)}) collective-permute-start(bf16[256,512]{1,0:T(8,128)(2,1)S(1)} %bitcast.120), channel_id=1, source_target_pairs={{4,0},{8,4},{12,8},{16,12},{20,16},{24,20},{28,24},{5,1},{9,5},{13... | collective-permute-start | bytes 786440 | tf_op jit(solution)/shard_map/ppermute | solution.py:13
  42.4 4.4 %collective-permute-start.1 = (bf16[256,512]{1,0:T(8,128)(2,1)S(1)}, bf16[256,512]{1,0:T(8,128)(2,1)S(1)}, u32[]{:S(2)}, u32[]{:S(2)}) collective-permute-start(bf16[256,512]{1,0:T(8,128)(2,1)S(1)} %bitcast.119), channel_id=1, source_target_pairs={{0,4},{4,8},{8,12},{12,16},{16,20},{20,24},{24,28},{1,5},{5,9},{9,... | collective-permute-start | bytes 786440 | tf_op jit(solution)/shard_map/ppermute | solution.py:13
  64.2 6.7 %copy-start.1 = (bf16[64,12,4,8,128]{4,3,2,1,0:T(8,128)(2,1)}, bf16[64,12,4,8,128]{4,3,2,1,0:T(8,128)(2,1)S(1)}, u32[]{:S(2)}) copy-start(bf16[64,12,4,8,128]{4,3,2,1,0:T(8,128)(2,1)S(1)} %get-tuple-element.16) | copy-start | bytes 18874372
  64.2 6.7 %copy-start.2 = (bf16[64,12,4,8,128]{4,3,2,1,0:T(8,128)(2,1)}, bf16[64,12,4,8,128]{4,3,2,1,0:T(8,128)(2,1)S(1)}, u32[]{:S(2)}) copy-start(bf16[64,12,4,8,128]{4,3,2,1,0:T(8,128)(2,1)S(1)} %get-tuple-element.17) | copy-start | bytes 18874372
  81.0 6.5 %collective-permute-start.2 = (bf16[256,1024]{1,0:T(8,128)(2,1)S(1)}, bf16[256,1024]{1,0:T(8,128)(2,1)S(1)}, u32[]{:S(2)}, u32[]{:S(2)}) collective-permute-start(bf16[256,1024]{1,0:T(8,128)(2,1)S(1)} %get-tuple-element.20), channel_id=1, source_target_pairs={{0,4},{4,8},{8,12},{12,16},{16,20},{20,24},{24,28},{1,5},{5,9},{9,... | collective-permute-start | bytes 1572872 | tf_op jit(solution)/shard_map/ppermute | solution.py:13
  86.0 5.8 %collective-permute-start.3 = (bf16[256,1024]{1,0:T(8,128)(2,1)S(1)}, bf16[256,1024]{1,0:T(8,128)(2,1)S(1)}, u32[]{:S(2)}, u32[]{:S(2)}) collective-permute-start(bf16[256,1024]{1,0:T(8,128)(2,1)S(1)} %get-tuple-element.21), channel_id=1, source_target_pairs={{4,0},{8,4},{12,8},{16,12},{20,16},{24,20},{28,24},{5,1},{9,5},{13... | collective-permute-start | bytes 1572872 | tf_op jit(solution)/shard_map/ppermute | solution.py:13
  91.7 6.1 %copy-start.16 = (bf16[64,4,96,1]{2,1,0,3:T(4,128)(2,1)S(1)}, bf16[64,4,96,1]{2,1,0,3:T(4,128)(2,1)}, u32[]{:S(2)}) copy-start(bf16[64,4,96,1]{2,1,0,3:T(4,128)(2,1)} %get-tuple-element.27) | copy-start | bytes 147460
  91.9 12.0 %slice-start = ((s8[6291456]{0:T(1024)(128)(4,1)}), s8[2097152]{0:T(1024)(128)(4,1)S(1)}, s32[]{:S(2)}) async-start(s8[6291456]{0:T(1024)(128)(4,1)} %bitcast.102), calls=%async_computation.3 | async-start | bytes 4194304
  93.2 37.6 %all-to-all-start.1 = ((bf16[3,4,64,1024]{3,2,0,1:T(8,128)(2,1)}), bf16[3,4,64,1024]{3,2,0,1:T(8,128)(2,1)}, u32[]{:S(2)}, u32[]{:S(2)}) async-start(bf16[3,4,64,1024]{3,2,0,1:T(8,128)(2,1)} %copy.35), calls=%async_computation.1 | async-start | bytes 3145728 | tf_op jit(solution)/shard_map/all_to_all | solution.py:152
  97.6 194.4 %all-reduce.2.cloned.1.call-start = ((), (), s32[]{:S(2)}) async-start(), calls=%async_computation.2 | async-start | bytes 8388608 | tf_op jit(solution)/shard_map/psum | solution.py:178
  97.8 6.0 %copy-start.15 = (bf16[64,4,96]{2,1,0:T(4,128)(2,1)S(1)}, bf16[64,4,96]{2,1,0:T(4,128)(2,1)}, u32[]{:S(2)}) copy-start(bf16[64,4,96]{2,1,0:T(4,128)(2,1)} %copy-done.14) | copy-start | bytes 147460
  97.9 6.0 %slice-start.1 = ((s8[6291456]{0:T(1024)(128)(4,1)}), s8[4194304]{0:T(1024)(128)(4,1)S(1)}, s32[]{:S(2)}) async-start(s8[6291456]{0:T(1024)(128)(4,1)} %bitcast.102), calls=%async_computation.4 | async-start | bytes 8388608
  105.6 26.8 %copy-start.10 = (bf16[768,512]{1,0:T(8,128)(2,1)S(1)}, bf16[768,512]{1,0:T(8,128)(2,1)}, u32[]{:S(2)}) copy-start(bf16[768,512]{1,0:T(8,128)(2,1)} %copy-done.9) | copy-start | bytes 2359300
  136.6 4.9 %copy-start.25 = (s32[768]{0:T(1024)S(1)}, s32[768]{0:T(1024)}, u32[]{:S(2)}) copy-start(s32[768]{0:T(1024)} %copy-done.24) | copy-start | bytes 9220
  136.6 4.9 %copy-start.27 = (f32[512]{0:T(512)S(1)}, f32[512]{0:T(512)}, u32[]{:S(2)}) copy-start(f32[512]{0:T(512)} %param.15) | copy-start | bytes 6148
  (15 other events, 36.2 us)
Sparse Core Ops, SparseCore 0:
  136.8 155.1 all-reduce.1
where the time goes:
time: 304 us; the launch traced here: 303 us
  waiting for transfers between devices  184 us (61%)
  matrix products  49.8 us (16%)
  local copies, waits for them, and re-layouts  25.1 us (8%)
  starting transfers between devices  21.8 us (7%)
  between operations  14.6 us (5%)
  other arithmetic  8.64 us (3%)
    psum x1, waiting for transfers between devices, shards(): weight_grads = lax.psum(local_grads, ('grid', 'sub'))  138 us
    all_to_all x1, waiting for transfers between devices, shards(): lax.all_to_all(home, 'sub', split_axis=1, concat_axis=1, tiled=True)  24.3 us
    unnamed x69, local copies, waits for them, and re-layouts  19.4 us
    all_to_all x1, waiting for transfers between devices, shards(): lax.all_to_all(packet, 'sub', split_axis=1, concat_axis=1, tiled=True)  17 us
    dot_general x1, matrix products, shards(): jnp.einsum('gjc,ce->gje', slot_onehot, recv_pair, preferred_element_type=...  11.4 us
    ppermute x4, starting transfers between devices, from_behind(): return lax.ppermute(block, axis, route)  10.8 us
    all_to_all x1, starting transfers between devices, shards(): lax.all_to_all(packet, 'sub', split_axis=1, concat_axis=1, tiled=True)  6.35 us
    dot_general x1, matrix products, shards(): jnp.einsum('sp,sd->pd', send_match.astype(jnp.float32), slot_back, precis...  6.08 us
  transfers between devices with their start and end apart: 7, of which 5 were waited for; matrix products, arithmetic and copies ran while one was open for 10% of the time, Pallas kernels for 0%

commit v1 on v0

--- a/solution.py
+++ b/solution.py
@@ -175,7 +175,7 @@
     local_grads = jnp.stack(
         [grad_wq, pair_grads[:, :model_width], pair_grads[:, model_width:], grad_wo]
     )
-    weight_grads = lax.psum(local_grads, ("grid", "sub"))
+    weight_grads = lax.psum(lax.psum(local_grads, "sub"), "grid")
     return (mesh_out, mesh_grad, grid_grad, weight_grads)
 
 

time: 304 us -> 400 us (1.32)
  waiting for transfers between devices: 184 us -> 278 us
    psum x1 -> x2, waiting for transfers between devices: 138 us -> 232 us  [shards(): weight_grads = lax.psum(lax.psum(local_grads, 'sub'), 'grid')]
    unnamed x69 -> x67, local copies, waits for them, and re-layouts: 19.4 us -> 19.4 us
  transfers between devices with their start and end apart: 7 -> 8, of which waited for: 5 -> 5; matrix products, arithmetic and copies ran while one was open for 10% -> 8% of each run, Pallas kernels for 0% -> 0%
where the time goes in v1:
time: 400 us; the launch traced here: 399 us
  waiting for transfers between devices  278 us (70%)
  matrix products  49.8 us (12%)
  local copies, waits for them, and re-layouts  25.1 us (6%)
  starting transfers between devices  21.9 us (5%)
  between operations  14.6 us (4%)
  other arithmetic  9.3 us (2%)
    psum x2, waiting for transfers between devices, shards(): weight_grads = lax.psum(lax.psum(local_grads, 'sub'), 'grid')  232 us
    all_to_all x1, waiting for transfers between devices, shards(): lax.all_to_all(home, 'sub', split_axis=1, concat_axis=1, tiled=True)  25 us
    unnamed x67, local copies, waits for them, and re-layouts  19.4 us
    all_to_all x1, waiting for transfers between devices, shards(): lax.all_to_all(packet, 'sub', split_axis=1, concat_axis=1, tiled=True)  17 us
    dot_general x1, matrix products, shards(): jnp.einsum('gjc,ce->gje', slot_onehot, recv_pair, preferred_element_type=...  11.4 us
    ppermute x4, starting transfers between devices, from_behind(): return lax.ppermute(block, axis, route)  11 us
  transfers between devices with their start and end apart: 8, of which 5 were waited for; matrix products, arithmetic and copies ran while one was open for 8% of the time, Pallas kernels for 0%

profile of v1, /device:TPU:0, one launch (start us, length us, event | category | flops | bytes accessed | tf_op | source)
XLA Modules:
  0.0 399.0 jit_solution(14096659698154937789)
XLA Ops:
  7.2 3.0 copy.27
  14.6 6.3 %all-to-all-start = ((bf16[3,4,64,512]{3,2,0,1:T(8,128)(2,1)}), bf16[3,4,64,512]{3,2,0,1:T(8,128)(2,1)S(1)}, u32[]{:S(2)}, u32[]{:S(2)}) async-start(bf16[3,4,64,512]{3,2,0,1:T(8,128)(2,1)} %copy.28), calls=%async_computation | async-start | bytes 1572864 | tf_op jit(solution)/shard_map/all_to_all | solution.py:63
  24.0 17.0 %all-to-all-done = bf16[3,4,64,512]{3,2,0,1:T(8,128)(2,1)S(1)} async-done(((bf16[3,4,64,512]{3,2,0,1:T(8,128)(2,1)}), bf16[3,4,64,512]{3,2,0,1:T(8,128)(2,1)S(1)}, u32[]{:S(2)}, u32[]{:S(2)}) %all-to-all-start) | async-done | bytes 786464 | tf_op jit(solution)/shard_map/all_to_all | solution.py:63
  42.4 3.2 collective-permute-start.1
  46.8 2.2 fusion.123
  49.0 11.4 %fusion.7 = bf16[64,96,1024]{2,1,0:T(8,128)(2,1)S(1)} fusion(s32[64,96]{1,0:T(8,128)} %param.22, bf16[768,1024,1]{1,0,2:T(8,128)(2,1)S(1)} %fusion.123), kind=kOutput, calls=%fused_computation.12 | convolution fusion | flops 9674686464 | bytes 14180352 | tf_op jit(solution)/shard_map/gjc,ce->gje/dot_general | solution.py:77
  60.5 3.7 slice_bitcast_fusion.1
  64.3 3.3 fusion.14
  67.6 3.3 fusion.8
  71.2 3.6 fusion.39
  75.8 3.5 fusion.38
  81.0 5.0 %collective-permute-start.2 = (bf16[256,1024]{1,0:T(8,128)(2,1)S(1)}, bf16[256,1024]{1,0:T(8,128)(2,1)S(1)}, u32[]{:S(2)}, u32[]{:S(2)}) collective-permute-start(bf16[256,1024]{1,0:T(8,128)(2,1)S(1)} %get-tuple-element.20), channel_id=1, source_target_pairs={{0,4},{4,8},{8,12},{12,16},{16,20},{20,24},{24,28},{1,5},{5,9},{9,... | collective-permute-start | bytes 1572872 | tf_op jit(solution)/shard_map/ppermute | solution.py:13
  87.5 4.2 %collective-permute-done.3 = bf16[256,1024]{1,0:T(8,128)(2,1)S(1)} collective-permute-done((bf16[256,1024]{1,0:T(8,128)(2,1)S(1)}, bf16[256,1024]{1,0:T(8,128)(2,1)S(1)}, u32[]{:S(2)}, u32[]{:S(2)}) %collective-permute-start.3) | collective-permute-done | bytes 524320 | tf_op jit(solution)/shard_map/ppermute | solution.py:13
  93.2 4.4 %all-to-all-start.1 = ((bf16[3,4,64,1024]{3,2,0,1:T(8,128)(2,1)}), bf16[3,4,64,1024]{3,2,0,1:T(8,128)(2,1)}, u32[]{:S(2)}, u32[]{:S(2)}) async-start(bf16[3,4,64,1024]{3,2,0,1:T(8,128)(2,1)} %copy.35), calls=%async_computation.1 | async-start | bytes 3145728 | tf_op jit(solution)/shard_map/all_to_all | solution.py:152
  97.7 4.7 %fusion.10 = f32[64,4,1,128]{3,2,1,0:T(1,128)S(1)} fusion(bf16[64,12,4,8,128]{4,3,2,1,0:T(8,128)(2,1)} %copy-done.2, bf16[64,4,96,1]{2,1,0,3:T(4,128)(2,1)S(1)} %copy-done.16), kind=kOutput, calls=%fused_computation.15 | convolution fusion | flops 6291456 | bytes 6471680 | tf_op jit(solution)/shard_map/gij,gjik->gik/dot_general | solution.py:96
  105.9 25.0 %all-to-all-done.1 = bf16[3,4,64,1024]{3,2,0,1:T(8,128)(2,1)} async-done(((bf16[3,4,64,1024]{3,2,0,1:T(8,128)(2,1)}), bf16[3,4,64,1024]{3,2,0,1:T(8,128)(2,1)}, u32[]{:S(2)}, u32[]{:S(2)}) %all-to-all-start.1) | async-done | bytes 1572896 | tf_op jit(solution)/shard_map/all_to_all | solution.py:152
  134.2 2.5 pad_maximum_fusion
  137.7 166.7 %all-reduce.3.cloned.1.call-done = f32[4,512,512]{2,1,0:T(8,128)} async-done(((f32[4,512,512]{2,1,0:T(8,128)}), f32[4,512,512]{2,1,0:T(8,128)}) %all-reduce.3.cloned.1.call-update) | async-done | bytes 4194320 | tf_op jit(solution)/shard_map/psum | solution.py:178
  306.8 2.7 fusion.93
  309.5 6.1 %fusion.28 = (f32[2048]{0:T(1024)S(1)}, f32[2048,512]{0,1:T(8,128)S(1)}) fusion(bf16[2048,512]{0,1:T(8,128)(2,1)S(1)} %copy-done.4, f32[512]{0:T(512)S(1)} %copy-done.27, f32[768,512]{1,0:T(8,128)S(1)} %fusion.93, s32[768]{0:T(1024)S(1)} %copy-done.25), kind=kOutput, calls=%fused_computation.36 | convolution fusion | flops 9669441536 | bytes 7877632 | tf_op jit(solution)/shard_map/sp,sd->pd/dot_general | solution.py:157
  315.6 2.5 fusion.27
  318.1 3.9 copy.37
  322.1 65.4 %all-reduce.5.cloned.1.call-done = f32[4,512,512]{2,1,0:T(8,128)} async-done(((f32[4,512,512]{2,1,0:T(8,128)}), f32[4,512,512]{2,1,0:T(8,128)}) %all-reduce.5.cloned.1.call-update) | async-done | bytes 4194320 | tf_op jit(solution)/shard_map/psum | solution.py:178
  387.5 4.6 %copy.107 = f32[4,512,512]{2,1,0:T(8,128)} copy(f32[4,512,512]{2,1,0:T(8,128)} %all-reduce.5.cloned.1.call-done) | data formatting | bytes 8388608
  (111 shorter events, 26.0 us)
Async XLA Ops:
  7.2 16.6 %copy-start = (bf16[512,512]{1,0:T(8,128)(2,1)S(1)}, bf16[512,512]{1,0:T(8,128)(2,1)}, u32[]{:S(2)}) copy-start(bf16[512,512]{1,0:T(8,128)(2,1)} %param.17) | copy-start | bytes 1572868
  10.8 10.2 %copy-start.6 = (bf16[64,512]{1,0:T(8,128)(2,1)S(1)}, bf16[64,512]{1,0:T(8,128)(2,1)}, u32[]{:S(2)}) copy-start(bf16[64,512]{1,0:T(8,128)(2,1)} %param.14) | copy-start | bytes 196612
  12.8 10.7 %copy-start.7 = (bf16[512,512]{1,0:T(8,128)(2,1)S(1)}, bf16[512,512]{1,0:T(8,128)(2,1)}, u32[]{:S(2)}) copy-start(bf16[512,512]{1,0:T(8,128)(2,1)} %param.20) | copy-start | bytes 1572868
  12.8 10.7 %copy-start.11 = (bf16[64,512]{1,0:T(8,128)(2,1)S(1)}, bf16[64,512]{1,0:T(8,128)(2,1)}, u32[]{:S(2)}) copy-start(bf16[64,512]{1,0:T(8,128)(2,1)} %param.25) | copy-start | bytes 196612
  13.7 10.1 %copy-start.18 = (f32[512]{0:T(512)S(1)}, f32[512]{0:T(512)}, u32[]{:S(2)}) copy-start(f32[512]{0:T(512)} %param.16) | copy-start | bytes 6148
  13.7 32.0 %copy-start.12 = (bf16[512,512]{1,0:T(8,128)(2,1)S(1)}, bf16[512,512]{1,0:T(8,128)(2,1)}, u32[]{:S(2)}) copy-start(bf16[512,512]{1,0:T(8,128)(2,1)} %param.19) | copy-start | bytes 1572868
  13.7 32.9 %copy-start.13 = (f32[64,384]{1,0:T(8,128)S(1)}, f32[64,384]{1,0:T(8,128)}, u32[]{:S(2)}) copy-start(f32[64,384]{1,0:T(8,128)} %param.21) | copy-start | bytes 294916
  13.7 33.1 %copy-start.17 = (s32[64,96]{1,0:T(8,128)S(1)}, s32[64,96]{1,0:T(8,128)}, u32[]{:S(2)}) copy-start(s32[64,96]{1,0:T(8,128)} %param.23) | copy-start | bytes 73732
  14.6 26.5 %all-to-all-start = ((bf16[3,4,64,512]{3,2,0,1:T(8,128)(2,1)}), bf16[3,4,64,512]{3,2,0,1:T(8,128)(2,1)S(1)}, u32[]{:S(2)}, u32[]{:S(2)}) async-start(bf16[3,4,64,512]{3,2,0,1:T(8,128)(2,1)} %copy.28), calls=%async_computation | async-start | bytes 1572864 | tf_op jit(solution)/shard_map/all_to_all | solution.py:63
  41.1 5.7 %collective-permute-start = (bf16[256,512]{1,0:T(8,128)(2,1)S(1)}, bf16[256,512]{1,0:T(8,128)(2,1)S(1)}, u32[]{:S(2)}, u32[]{:S(2)}) collective-permute-start(bf16[256,512]{1,0:T(8,128)(2,1)S(1)} %bitcast.120), channel_id=1, source_target_pairs={{4,0},{8,4},{12,8},{16,12},{20,16},{24,20},{28,24},{5,1},{9,5},{13... | collective-permute-start | bytes 786440 | tf_op jit(solution)/shard_map/ppermute | solution.py:13
  42.4 4.4 %collective-permute-start.1 = (bf16[256,512]{1,0:T(8,128)(2,1)S(1)}, bf16[256,512]{1,0:T(8,128)(2,1)S(1)}, u32[]{:S(2)}, u32[]{:S(2)}) collective-permute-start(bf16[256,512]{1,0:T(8,128)(2,1)S(1)} %bitcast.119), channel_id=1, source_target_pairs={{0,4},{4,8},{8,12},{12,16},{16,20},{20,24},{24,28},{1,5},{5,9},{9,... | collective-permute-start | bytes 786440 | tf_op jit(solution)/shard_map/ppermute | solution.py:13
  64.2 6.7 %copy-start.1 = (bf16[64,12,4,8,128]{4,3,2,1,0:T(8,128)(2,1)}, bf16[64,12,4,8,128]{4,3,2,1,0:T(8,128)(2,1)S(1)}, u32[]{:S(2)}) copy-start(bf16[64,12,4,8,128]{4,3,2,1,0:T(8,128)(2,1)S(1)} %get-tuple-element.16) | copy-start | bytes 18874372
  64.2 6.7 %copy-start.2 = (bf16[64,12,4,8,128]{4,3,2,1,0:T(8,128)(2,1)}, bf16[64,12,4,8,128]{4,3,2,1,0:T(8,128)(2,1)S(1)}, u32[]{:S(2)}) copy-start(bf16[64,12,4,8,128]{4,3,2,1,0:T(8,128)(2,1)S(1)} %get-tuple-element.17) | copy-start | bytes 18874372
  81.0 6.5 %collective-permute-start.2 = (bf16[256,1024]{1,0:T(8,128)(2,1)S(1)}, bf16[256,1024]{1,0:T(8,128)(2,1)S(1)}, u32[]{:S(2)}, u32[]{:S(2)}) collective-permute-start(bf16[256,1024]{1,0:T(8,128)(2,1)S(1)} %get-tuple-element.20), channel_id=1, source_target_pairs={{0,4},{4,8},{8,12},{12,16},{16,20},{20,24},{24,28},{1,5},{5,9},{9,... | collective-permute-start | bytes 1572872 | tf_op jit(solution)/shard_map/ppermute | solution.py:13
  86.0 5.8 %collective-permute-start.3 = (bf16[256,1024]{1,0:T(8,128)(2,1)S(1)}, bf16[256,1024]{1,0:T(8,128)(2,1)S(1)}, u32[]{:S(2)}, u32[]{:S(2)}) collective-permute-start(bf16[256,1024]{1,0:T(8,128)(2,1)S(1)} %get-tuple-element.21), channel_id=1, source_target_pairs={{4,0},{8,4},{12,8},{16,12},{20,16},{24,20},{28,24},{5,1},{9,5},{13... | collective-permute-start | bytes 1572872 | tf_op jit(solution)/shard_map/ppermute | solution.py:13
  91.7 5.9 %copy-start.16 = (bf16[64,4,96,1]{2,1,0,3:T(4,128)(2,1)S(1)}, bf16[64,4,96,1]{2,1,0,3:T(4,128)(2,1)}, u32[]{:S(2)}) copy-start(bf16[64,4,96,1]{2,1,0,3:T(4,128)(2,1)} %get-tuple-element.27) | copy-start | bytes 147460
  91.9 11.8 %slice-start = ((s8[6291456]{0:T(1024)(128)(4,1)}), s8[2097152]{0:T(1024)(128)(4,1)S(1)}, s32[]{:S(2)}) async-start(s8[6291456]{0:T(1024)(128)(4,1)} %bitcast.102), calls=%async_computation.4 | async-start | bytes 4194304
  93.2 37.6 %all-to-all-start.1 = ((bf16[3,4,64,1024]{3,2,0,1:T(8,128)(2,1)}), bf16[3,4,64,1024]{3,2,0,1:T(8,128)(2,1)}, u32[]{:S(2)}, u32[]{:S(2)}) async-start(bf16[3,4,64,1024]{3,2,0,1:T(8,128)(2,1)} %copy.35), calls=%async_computation.1 | async-start | bytes 3145728 | tf_op jit(solution)/shard_map/all_to_all | solution.py:152
  97.6 206.8 %all-reduce.3.cloned.1.call-start = ((), (), s32[]{:S(2)}) async-start(), calls=%async_computation.2 | async-start | bytes 8388608 | tf_op jit(solution)/shard_map/psum | solution.py:178
  97.7 6.0 %copy-start.15 = (bf16[64,4,96]{2,1,0:T(4,128)(2,1)S(1)}, bf16[64,4,96]{2,1,0:T(4,128)(2,1)}, u32[]{:S(2)}) copy-start(bf16[64,4,96]{2,1,0:T(4,128)(2,1)} %copy-done.14) | copy-start | bytes 147460
  97.7 6.0 %slice-start.1 = ((s8[6291456]{0:T(1024)(128)(4,1)}), s8[4194304]{0:T(1024)(128)(4,1)S(1)}, s32[]{:S(2)}) async-start(s8[6291456]{0:T(1024)(128)(4,1)} %bitcast.102), calls=%async_computation.5 | async-start | bytes 8388608
  105.4 27.0 %copy-start.10 = (bf16[768,512]{1,0:T(8,128)(2,1)S(1)}, bf16[768,512]{1,0:T(8,128)(2,1)}, u32[]{:S(2)}) copy-start(bf16[768,512]{1,0:T(8,128)(2,1)} %copy-done.9) | copy-start | bytes 2359300
  136.7 250.8 %all-reduce.5.cloned.1.call-start = ((), (), s32[]{:S(2)}) async-start(), calls=%async_computation.3 | async-start | bytes 8388608 | tf_op jit(solution)/shard_map/psum | solution.py:178
  304.4 5.1 %copy-start.27 = (f32[512]{0:T(512)S(1)}, f32[512]{0:T(512)}, u32[]{:S(2)}) copy-start(f32[512]{0:T(512)} %param.15) | copy-start | bytes 6148
  (15 other events, 40.8 us)
Sparse Core Ops, SparseCore 0:
  136.8 167.5 all-reduce.2
  307.7 79.7 all-reduce.4
